TPU v7x, 128 devices: a whole 4x4x4 slice. The times are simulated.
128 devices in a mesh: sky: 32 (over y, z, core), band: 4 (over x).
Axes of the slice: x: 4, y: 4, z: 4, core: 2. Of those that a mesh axis runs over, the one named last changes fastest.
Arguments:
- exposures: bfloat16 [32, 4, 1024, 1024], P('sky', 'band'), may hold values from -6 to 6
- inv_variance: bfloat16 [32, 4, 1024, 1024], P('sky', 'band'), may hold values from 0.25 to 4
- mask_planes: int32 [32, 4, 2, 35], P('sky', 'band'), may hold values from 0 to 1073741823, as said below
- sky_columns: int32 [32, 4, 8], replicated, may hold values from 0 to 31, as said below
- basis_rows: float32 [9, 25], replicated, may hold values from -1 to 1
- basis_cols: float32 [9, 25], replicated, may hold values from -1 to 1
- match_coeffs: float32 [32, 4, 9], P('sky', 'band'), may hold values from -2 to 2
- detect_taps: float32 [4, 31], P('band'), may hold values from 0.05 to 0.3
Outputs:
- difference: bfloat16 [32, 4, 1024, 1024], P('sky', 'band')
- detection: float32 [1024, 4096], P('band', 'sky')
Inputs may be any that keep to these rules, and one draw needn't show every extreme that they name: Each row sky_columns[e, b] holds 8 consecutive sky tile columns in order, counted modulo 32; every sky tile column is covered by some exposure of every band. Bit j of mask_planes[e, b, 0, w] marks pixel column 30 w + j of that exposure as bad and bit j of mask_planes[e, b, 1, w] pixel row 30 w + j; bits past 1024 are ignored. In every draw some word has all 30 bits set.
All inputs are finite; a program needn't handle non-finite values.
Results may differ from a plain program's by a relative error of at most 0.0095.
Values may be sent and summed in bfloat16 or wider, within the bound.
A program may use at most 128 MiB of HBM per device.

v0:
```python
import jax
import jax.numpy as jnp
from jax import lax
from jax.sharding import PartitionSpec as P

TILE = 128
NB = 9
TAPS = 25
DTAPS = 31


def with_halo(block, sides, width):
    for axis, dim in sides:
        count = lax.axis_size(axis)
        forward = [(i, i + 1) for i in range(count - 1)]
        forward.append((count - 1, 0))
        backward = [(target, source) for source, target in forward]
        low = lax.ppermute(
            lax.slice_in_dim(block, block.shape[dim] - width, None, axis=dim), axis, forward
        )
        high = lax.ppermute(lax.slice_in_dim(block, 0, width, axis=dim), axis, backward)
        block = jnp.concatenate([low, block, high], axis=dim)
    return block


def cut_along(value, dim, length):
    dims = value.shape
    pieces = value.reshape(*dims[:dim], length, dims[dim] // length, *dims[dim + 1 :])
    return jnp.moveaxis(pieces, dim, 0)


def sum_at_owner(value, axis, dim):
    pieces = cut_along(value, dim, lax.axis_size(axis))
    arrived = lax.all_to_all(pieces, axis, split_axis=0, concat_axis=0, tiled=True)
    return arrived.sum(axis=0)


def band_matrix(tap_rows, window_width):
    offsets = (
        jnp.arange(window_width, dtype=jnp.int32)[:, None]
        - jnp.arange(TILE, dtype=jnp.int32)[None, :]
    )
    selector = (
        offsets[:, :, None] == jnp.arange(tap_rows.shape[1], dtype=jnp.int32)[None, None, :]
    ).astype(jnp.float32)
    return jnp.einsum(
        "wtl,kl->kwt", selector, tap_rows.astype(jnp.float32), precision=lax.Precision.HIGHEST
    ).astype(jnp.bfloat16)


def keep_pixels(planes, side_length):
    places = jnp.arange(side_length, dtype=jnp.int32)
    column_bits = jnp.bitwise_and(jnp.right_shift(planes[0][places // 30], places % 30), 1)
    row_bits = jnp.bitwise_and(jnp.right_shift(planes[1][places // 30], places % 30), 1)
    return jnp.logical_and(row_bits[:, None] == 0, column_bits[None, :] == 0)


def psf_match(picture, column_taps, row_taps):
    side_length = picture.shape[1]
    block_count = side_length // TILE
    margin = TAPS // 2
    width_full = TILE + 2 * margin
    padded = jnp.pad(picture, ((0, 0), (margin, margin)))
    blocks = jnp.stack(
        [
            padded[:, TILE * block_index : TILE * block_index + width_full]
            for block_index in range(block_count)
        ],
        0,
    )
    column_band = band_matrix(column_taps, width_full)
    column_pass = jnp.einsum(
        "jyw,kwt->kyjt", blocks, column_band, preferred_element_type=jnp.float32
    )
    column_pass = column_pass.reshape(NB, side_length, side_length).astype(jnp.bfloat16)
    row_padded = jnp.pad(column_pass, ((0, 0), (margin, margin), (0, 0)))
    row_blocks = jnp.stack(
        [
            row_padded[:, TILE * block_index : TILE * block_index + width_full, :]
            for block_index in range(block_count)
        ],
        0,
    )
    row_band = band_matrix(row_taps, width_full)
    summed = jnp.einsum("ikwx,kwt->itx", row_blocks, row_band, preferred_element_type=jnp.float32)
    return summed.reshape(side_length, side_length).astype(jnp.bfloat16)


def average_pieces(pieces):
    matched_in, weight_in = pieces
    weight_float = weight_in.astype(jnp.float32)
    numer = jnp.sum(weight_float * matched_in.astype(jnp.float32), axis=1)
    denom = jnp.sum(weight_float, axis=1)
    return (numer / jnp.maximum(denom, 1.0)).astype(jnp.bfloat16)


def subtract_template(template, matched, own_columns, side_length, sky_count):
    gathered = lax.all_gather(template, "sky", axis=1, tiled=True).reshape(
        side_length, sky_count, TILE
    )
    picked = jnp.take(gathered, own_columns, axis=1).reshape(side_length, side_length)
    return (matched.astype(jnp.float32) - picked.astype(jnp.float32)).astype(jnp.bfloat16)


def body(
    exposures,
    inv_variance,
    mask_planes,
    sky_columns,
    basis_rows,
    basis_cols,
    match_coeffs,
    detect_taps,
):
    picture = exposures[0, 0]
    side_length = picture.shape[0]
    block_count = side_length // TILE
    sky_count = lax.axis_size("sky")
    own_sky = lax.axis_index("sky")
    own_band = lax.axis_index("band")
    column_taps = (match_coeffs[0, 0][:, None] * basis_cols).astype(jnp.bfloat16)
    matched = psf_match(picture, column_taps, basis_rows.astype(jnp.bfloat16))
    keep = keep_pixels(mask_planes[0, 0], side_length)
    variance_inv = inv_variance[0, 0]
    weight = jnp.where(keep, variance_inv, jnp.zeros_like(variance_inv))
    own_columns = sky_columns[own_sky, own_band]
    empty_slots = jnp.zeros((side_length, sky_count, TILE), jnp.bfloat16)
    send_matched = empty_slots.at[:, own_columns, :].set(
        matched.reshape(side_length, block_count, TILE)
    )
    send_weight = empty_slots.at[:, own_columns, :].set(
        weight.reshape(side_length, block_count, TILE)
    )
    template = average_pieces(
        (
            lax.all_to_all(send_matched, "sky", split_axis=1, concat_axis=1, tiled=True),
            lax.all_to_all(send_weight, "sky", split_axis=1, concat_axis=1, tiled=True),
        )
    )
    difference = subtract_template(template, matched, own_columns, side_length, sky_count)
    margin = DTAPS // 2
    width_full = TILE + 2 * margin
    filter_band = band_matrix(detect_taps.astype(jnp.bfloat16), width_full)[0]
    widened = with_halo(template, (("sky", 1),), margin)
    smoothed = jnp.dot(widened, filter_band, preferred_element_type=jnp.float32).astype(
        jnp.bfloat16
    )
    smooth_padded = jnp.pad(smoothed, ((margin, margin), (0, 0)))
    smooth_blocks = jnp.stack(
        [
            smooth_padded[TILE * block_index : TILE * block_index + width_full]
            for block_index in range(block_count)
        ],
        0,
    )
    filtered = jnp.einsum(
        "iwx,wt->itx", smooth_blocks, filter_band, preferred_element_type=jnp.float32
    ).reshape(side_length, TILE)
    power = filtered * filtered
    detection = sum_at_owner(power, "band", 0)
    return (difference[None, None], detection)


def solution(mesh):
    in_specs = (
        P("sky", "band", None, None),
        P("sky", "band", None, None),
        P("sky", "band", None, None),
        P(),
        P(),
        P(),
        P("sky", "band", None),
        P("band", None),
    )
    out_specs = (P("sky", "band", None, None), P("band", "sky"))
    return jax.shard_map(body, mesh=mesh, in_specs=in_specs, out_specs=out_specs, check_vma=False)
```

profile of v0, /device:TPU:1, one launch (start us, length us, event | category | flops | bytes accessed | tf_op | source)
XLA Modules:
  0.0 444.7 jit_solution(8928743750772134446)
XLA Ops:
  7.2 2.9 copy.63
  11.6 9.2 %convolution_convert_fusion = bf16[9,128,8,1024]{3,1,2,0:T(8,128)(2,1)} fusion(bf16[8,1024,152]{1,2,0:T(8,128)(2,1)S(1)} %fusion.34, bf16[9,152,128,1]{2,0,1,3:T(8,128)(2,1)S(1)} %fusion.19), kind=kOutput, calls=%fused_computation.8 | convolution fusion | flops 2878341120 | bytes 21714944 | tf_op jit(solution)/shard_map/jyw,kwt->kyjt/dot_general | solution.py:72
  20.8 24.6 %copy.65 = bf16[9,1024,1024]{2,1,0:T(8,128)(2,1)} copy(bf16[9,1024,1024]{1,2,0:T(8,128)(2,1)} %bitcast.238) | data formatting | bytes 37748736 | tf_op jit(solution)/shard_map/convert_element_type | solution.py:75
  45.4 4.3 fusion.2
  49.8 3.8 copy-done.2
  53.6 2.5 fusion.10
  58.5 2.5 fusion.8
  61.0 2.5 fusion.7
  71.4 9.9 %bitcast_convert_fusion = bf16[128,8,1024]{2,0,1:T(8,128)(2,1)S(1)} fusion(bf16[8,9,152,1024]{3,2,1,0:T(8,128)(2,1)} %fusion.4, bf16[9,152,128]{2,0,1:T(8,128)(2,1)S(1)} %fusion.20), kind=kOutput, calls=%fused_computation.9 | convolution fusion | flops 2869952512 | bytes 24860672 | tf_op jit(solution)/shard_map/ikwx,kwt->itx/dot_general | solution.py:85
  83.8 5.1 %broadcast_in_dim.18.clone.1 = bf16[1024,32,128]{2,0,1:T(8,128)(2,1)} broadcast(bf16[]{:T(256)} %constant.31.clone.1), dimensions={} | broadcast | bytes 8388610 | tf_op jit(solution)/shard_map/broadcast_in_dim | solution.py:127
  88.9 5.7 %scatter_fusion.1 = bf16[1024,32,128]{2,0,1:T(8,128)(2,1)} fusion(bf16[1024,32,128]{2,0,1:T(8,128)(2,1)} %broadcast_in_dim.18.clone.1, s32[8]{0:T(128)S(1)} %fusion.61, bf16[8,1024,128]{2,1,0:T(8,128)(2,1)} %bitcast.250), kind=kCustom, calls=%fused_computation.2 | custom fusion | bytes 6291488 | tf_op jit(solution)/shard_map/scatter | solution.py:128
  94.6 9.6 %all-to-all-start.1 = ((bf16[1024,32,128]{2,0,1:T(8,128)(2,1)}), bf16[1024,32,128]{2,0,1:T(8,128)(2,1)}, u32[]{:S(2)}, u32[]{:S(2)}) async-start(bf16[1024,32,128]{2,0,1:T(8,128)(2,1)} %scatter_fusion.1), calls=%async_computation.1 | async-start | bytes 16777216 | tf_op jit(solution)/shard_map/all_to_all | solution.py:136
  109.1 4.5 %compare_select_fusion.2 = s32[1024,1]{0,1:T(1,128)S(1)} fusion(s32[]{:T(128)} %bitcast.97, s32[]{:T(128)} %bitcast.98, s32[]{:T(128)} %bitcast.99, s32[]{:T(128)} %bitcast.100, s32[]{:T(128)} %bitcast.101, s32[]{:T(128)} %bitcast.103, s32[]{:T(128)} %bitcast.102), kind=kLoop, calls=%fused_computation.125 | loop fusion | flops 23552 | bytes 4124 | tf_op jit(solution)/shard_map/gather | solution.py:53
  115.0 4.4 compare_select_fusion.1
  119.5 17.3 %fusion.49 = pred[8,128]{1,0:T(8,128)(4,1)S(1)} fusion(pred[1024]{0:T(1024)(128)(4,1)S(1)} %compare_reduce_fusion, pred[1024]{0:T(1024)(128)(4,1)S(1)} %compare_reduce_fusion.1, pred[1024]{0:T(1024)(128)(4,1)S(1)} %compare_reduce_fusion.2, pred[1024]{0:T(1024)(128)(4,1)S(1)} %compare_reduce_fusion.3, pred[1024]{0:T(1024)(128)(4,1)S(1)} %compare_reduce_fusion.4, ...), kind=kLoop, calls=%fused_computation.147 | loop fusion | flops 39936 | bytes 33904 | tf_op jit(solution)/shard_map/eq | solution.py:55
  136.8 17.6 %fusion.46 = pred[1024]{0:T(1024)(128)(4,1)S(1)} fusion(pred[1024]{0:T(1024)(128)(4,1)S(1)} %compare_reduce_fusion, pred[1024]{0:T(1024)(128)(4,1)S(1)} %compare_reduce_fusion.1, pred[1024]{0:T(1024)(128)(4,1)S(1)} %compare_reduce_fusion.2, pred[1024]{0:T(1024)(128)(4,1)S(1)} %compare_reduce_fusion.3, pred[1024]{0:T(1024)(128)(4,1)S(1)} %compare_reduce_fusion.4, ...), kind=kLoop, calls=%fused_computation.144 | loop fusion | flops 37888 | bytes 33904 | tf_op jit(solution)/shard_map/eq | solution.py:55
  156.4 5.1 %broadcast_in_dim.18.clone = bf16[1024,32,128]{2,0,1:T(8,128)(2,1)} broadcast(bf16[]{:T(256)} %constant.31.clone.1), dimensions={} | broadcast | bytes 8388610 | tf_op jit(solution)/shard_map/broadcast_in_dim | solution.py:127
  161.5 5.8 %scatter_fusion = bf16[1024,32,128]{2,0,1:T(8,128)(2,1)} fusion(bf16[1024,32,128]{2,0,1:T(8,128)(2,1)} %broadcast_in_dim.18.clone, s32[8]{0:T(128)S(1)} %fusion.61, bf16[8,1024,128]{2,1,0:T(8,128)(2,1)} %fusion.16), kind=kCustom, calls=%fused_computation.1 | custom fusion | bytes 6291488 | tf_op jit(solution)/shard_map/scatter | solution.py:131
  167.3 45.5 %all-to-all-done.1 = bf16[1024,32,128]{2,0,1:T(8,128)(2,1)} async-done(((bf16[1024,32,128]{2,0,1:T(8,128)(2,1)}), bf16[1024,32,128]{2,0,1:T(8,128)(2,1)}, u32[]{:S(2)}, u32[]{:S(2)}) %all-to-all-start.1) | async-done | bytes 8388640 | tf_op jit(solution)/shard_map/all_to_all | solution.py:136
  212.8 117.1 %all_to_all.15 = bf16[1024,32,128]{2,0,1:T(8,128)(2,1)} all-to-all(bf16[1024,32,128]{2,0,1:T(8,128)(2,1)} %scatter_fusion), channel_id=1, replica_groups=mesh['sky'=32,'band'=4] {'sky'}, dimensions={1} | all-to-all | bytes 16777216 | tf_op jit(solution)/shard_map/all_to_all | solution.py:137
  329.9 9.0 %convert_reduce_fusion = (f32[1024,128]{1,0:T(8,128)S(1)}, f32[1024,128]{1,0:T(8,128)S(1)}) fusion(bf16[1024,32,128]{2,0,1:T(8,128)(2,1)} %all_to_all.15, bf16[1024,32,128]{2,0,1:T(8,128)(2,1)} %all-to-all-done.1), kind=kLoop, calls=%fused_computation.3 | loop fusion | flops 20709376 | bytes 17825792 | tf_op jit(solution)/shard_map/reduce_sum | solution.py:93
  341.4 3.0 copy.78
  344.5 2.8 collective-permute-done.1
  349.9 4.0 all-to-all-start.2
  354.0 6.8 %all-to-all-done.2 = f32[4,256,128]{2,1,0:T(8,128)S(1)} async-done(((f32[4,256,128]{2,1,0:T(8,128)}), f32[4,256,128]{2,1,0:T(8,128)S(1)}, u32[]{:S(2)}, u32[]{:S(2)}) %all-to-all-start.2) | async-done | bytes 524320 | tf_op jit(solution)/shard_map/all_to_all | solution.py:34
  361.5 36.1 %all-gather.2.cloned.1.call-done = bf16[1024,4096]{1,0:T(8,128)(2,1)} async-done(((bf16[1024,128]{1,0:T(8,128)(2,1)}), bf16[1024,4096]{1,0:T(8,128)(2,1)}) %all-gather.2.cloned.1.call-update) | async-done | bytes 8388624 | tf_op jit(solution)/shard_map/all_gather | solution.py:98
  397.6 11.9 %copy.75 = bf16[1024,4096]{0,1:T(8,128)(2,1)} copy(bf16[1024,4096]{1,0:T(8,128)(2,1)} %all-gather.2.cloned.1.call-done) | data formatting | bytes 16777216 | tf_op jit(solution)/shard_map/all_gather | solution.py:98
  409.5 11.9 %copy.76 = bf16[1024,32,128]{2,0,1:T(8,128)(2,1)} copy(bf16[1024,32,128]{0,2,1:T(8,128)(2,1)} %bitcast.239) | data formatting | bytes 16777216 | tf_op jit(solution)/shard_map/reshape | solution.py:98
  421.4 5.5 %gather_fusion = bf16[8,1024,128]{2,1,0:T(8,128)(2,1)} fusion(bf16[1024,32,128]{2,0,1:T(8,128)(2,1)} %copy.76, s32[1024]{0:T(1024)S(1)} %pad_clamp_fusion), kind=kCustom, calls=%fused_computation | custom fusion | bytes 4194336 | tf_op jit(solution)/shard_map/jit(_take)/gather | solution.py:101
  426.9 2.9 copy.77
  429.8 4.1 subtract_convert_fusion
  433.9 3.9 copy.79
  (94 shorter events, 28.4 us)
Async XLA Ops:
  7.2 76.4 %copy-start = (s32[32,4,8]{0,2,1:T(8,128)S(1)}, s32[32,4,8]{0,2,1:T(8,128)}, u32[]{:S(2)}) copy-start(s32[32,4,8]{0,2,1:T(8,128)} %param.11) | copy-start | bytes 12292
  10.3 0.7 copy-start.5
  10.3 0.7 copy-start.6
  45.4 8.2 %copy-start.2 = (bf16[9,1024,1024]{2,1,0:T(8,128)(2,1)S(1)}, bf16[9,1024,1024]{2,1,0:T(8,128)(2,1)}, u32[]{:S(2)}) copy-start(bf16[9,1024,1024]{2,1,0:T(8,128)(2,1)} %copy.65) | copy-start | bytes 56623108
  68.4 2.4 copy-start.7
  94.6 118.2 %all-to-all-start.1 = ((bf16[1024,32,128]{2,0,1:T(8,128)(2,1)}), bf16[1024,32,128]{2,0,1:T(8,128)(2,1)}, u32[]{:S(2)}, u32[]{:S(2)}) async-start(bf16[1024,32,128]{2,0,1:T(8,128)(2,1)} %scatter_fusion.1), calls=%async_computation.1 | async-start | bytes 16777216 | tf_op jit(solution)/shard_map/all_to_all | solution.py:136
  104.2 3.4 copy-start.4
  104.3 293.3 %all-gather.2.cloned.1.call-start = ((), (), s32[]{:S(2)}) async-start(), calls=%async_computation.3 | async-start | bytes 8650752 | tf_op jit(solution)/shard_map/all_gather | solution.py:98
  329.9 10.2 %copy-start.8 = (f32[1,31]{1,0:T(1,128)S(1)}, f32[1,31]{1,0:T(1,128)}, u32[]{:S(2)}) copy-start(f32[1,31]{1,0:T(1,128)} %param.15) | copy-start | bytes 376
  339.7 0.9 copy-start.3
  340.8 3.7 collective-permute-start
  341.1 6.1 %collective-permute-start.1 = (bf16[1024,15]{1,0:T(8,128)(2,1)S(1)}, bf16[1024,15]{1,0:T(8,128)(2,1)}, u32[]{:S(2)}, u32[]{:S(2)}) collective-permute-start(bf16[1024,15]{1,0:T(8,128)(2,1)S(1)} %get-tuple-element.11), channel_id=1, source_target_pairs={{4,0},{8,4},{12,8},{16,12},{20,16},{24,20},{28,24},{32,28},{36,32}... | collective-permute-start | bytes 92168 | tf_op jit(solution)/shard_map/ppermute | solution.py:21
  349.9 11.0 %all-to-all-start.2 = ((f32[4,256,128]{2,1,0:T(8,128)}), f32[4,256,128]{2,1,0:T(8,128)S(1)}, u32[]{:S(2)}, u32[]{:S(2)}) async-start(f32[4,256,128]{2,1,0:T(8,128)} %bitcast.124), calls=%async_computation.2 | async-start | bytes 1048576 | tf_op jit(solution)/shard_map/all_to_all | solution.py:34
  429.8 8.1 %copy-start.1 = (s32[32,4,8]{0,2,1:T(8,128)S(1)}, s32[32,4,8]{0,2,1:T(8,128)}, u32[]{:S(2)}) copy-start(s32[32,4,8]{0,2,1:T(8,128)} %param.11) | copy-start | bytes 12292
Sparse Core Ops, SparseCore 0:
  339.9 57.6 all-gather.1
where the time goes:
time: 447 us; the launch traced here: 445 us
  local copies, waits for them, and re-layouts  123 us (28%)
  blocking collectives  117 us (26%)
  waiting for transfers between devices  91.2 us (20%)
  other arithmetic  61.9 us (14%)
  matrix products  23.2 us (5%)
  starting transfers between devices  14.3 us (3%)
  between operations  14.3 us (3%)
    all_to_all x1, blocking collectives, body(): lax.all_to_all(send_weight, 'sky', split_axis=1, concat_axis=1, tiled=True)  117 us
    all_to_all x1, waiting for transfers between devices, body(): lax.all_to_all(send_matched, 'sky', split_axis=1, concat_axis=1, tiled=True)  45.5 us
    all_gather x1, waiting for transfers between devices, subtract_template(): lax.all_gather(template, 'sky', axis=1, tiled=True)  36.1 us
    eq x2, other arithmetic, keep_pixels(): return jnp.logical_and(row_bits[:, None] == 0, column_bits[None, :] == 0)  34.9 us
    unnamed x43, local copies, waits for them, and re-layouts  33.6 us
    convert_element_type x1, local copies, waits for them, and re-layouts, psf_match(): column_pass.reshape(NB, side_length, side_length).astype(jnp.bfloat16)  24.6 us
    all_gather x1, local copies, waits for them, and re-layouts, subtract_template(): lax.all_gather(template, 'sky', axis=1, tiled=True)  11.9 us
    reshape x1, local copies, waits for them, and re-layouts, subtract_template(): lax.all_gather(template, 'sky', axis=1, tiled=True)  11.9 us
  transfers between devices with their start and end apart: 5, of which 5 were waited for; matrix products, arithmetic and copies ran while one was open for 16% of the time, Pallas kernels for 0%

commit v1 on v0

--- a/solution.py
+++ b/solution.py
@@ -95,9 +95,9 @@
 
 
 def subtract_template(template, matched, own_columns, side_length, sky_count):
-    gathered = lax.all_gather(template, "sky", axis=1, tiled=True).reshape(
-        side_length, sky_count, TILE
-    )
+    gathered = jnp.concatenate(
+        lax.all_to_all(jnp.stack([template] * lax.axis_size("sky")), "sky", 0, 0), axis=1
+    ).reshape(side_length, sky_count, TILE)
     picked = jnp.take(gathered, own_columns, axis=1).reshape(side_length, side_length)
     return (matched.astype(jnp.float32) - picked.astype(jnp.float32)).astype(jnp.bfloat16)
 

time: 447 us -> 534 us (1.19)
  the two profiles are of different devices: /device:TPU:1 before, /device:TPU:32 now
where the time goes in v1:
time: 534 us; the launch traced here: 532 us
  waiting for transfers between devices  307 us (57%)
  local copies, waits for them, and re-layouts  104 us (19%)
  other arithmetic  62.1 us (12%)
  matrix products  22.6 us (4%)
  starting transfers between devices  21.5 us (4%)
  blocking collectives  13.8 us (3%)
    all_to_all x1, waiting for transfers between devices, body(): lax.all_to_all(send_weight, 'sky', split_axis=1, concat_axis=1, tiled=True)  123 us
    all_to_all x1, waiting for transfers between devices, subtract_template(): lax.all_to_all(jnp.stack([template] * lax.axis_size('sky')), 'sky', 0, 0)  120 us
    all_to_all x1, waiting for transfers between devices, body(): lax.all_to_all(send_matched, 'sky', split_axis=1, concat_axis=1, tiled=True)  61.3 us
    eq x2, other arithmetic, keep_pixels(): return jnp.logical_and(row_bits[:, None] == 0, column_bits[None, :] == 0)  34.9 us
    unnamed x41, local copies, waits for them, and re-layouts  33.5 us
    convert_element_type x1, local copies, waits for them, and re-layouts, psf_match(): column_pass.reshape(NB, side_length, side_length).astype(jnp.bfloat16)  24.6 us
    all_to_all x1, blocking collectives, sum_at_owner(): lax.all_to_all(pieces, axis, split_axis=0, concat_axis=0, tiled=True)  13.8 us
    scatter x2, local copies, waits for them, and re-layouts, body(): empty_slots.at[:, own_columns, :]  11.5 us
  transfers between devices with their start and end apart: 5, of which 4 were waited for; matrix products, arithmetic and copies ran while one was open for 13% of the time, Pallas kernels for 0%

profile of v1, /device:TPU:32, one launch (start us, length us, event | category | flops | bytes accessed | tf_op | source)
XLA Modules:
  0.0 532.1 jit_solution(11633801968990733470)
XLA Ops:
  0.7 2.9 copy.45
  5.1 9.2 %convolution_convert_fusion = bf16[9,128,8,1024]{3,1,2,0:T(8,128)(2,1)} fusion(bf16[8,1024,152]{1,2,0:T(8,128)(2,1)S(1)} %fusion.34, bf16[9,152,128,1]{2,0,1,3:T(8,128)(2,1)S(1)} %fusion.19), kind=kOutput, calls=%fused_computation.8 | convolution fusion | flops 2878341120 | bytes 21714944 | tf_op jit(solution)/shard_map/jyw,kwt->kyjt/dot_general | solution.py:72
  14.3 24.6 %copy.47 = bf16[9,1024,1024]{2,1,0:T(8,128)(2,1)} copy(bf16[9,1024,1024]{1,2,0:T(8,128)(2,1)} %bitcast.238) | data formatting | bytes 37748736 | tf_op jit(solution)/shard_map/convert_element_type | solution.py:75
  38.9 4.3 fusion.2
  43.2 3.8 copy-done.2
  47.1 2.5 fusion.10
  52.0 2.5 fusion.8
  54.5 2.5 fusion.7
  64.9 9.9 %bitcast_convert_fusion = bf16[128,8,1024]{2,0,1:T(8,128)(2,1)S(1)} fusion(bf16[8,9,152,1024]{3,2,1,0:T(8,128)(2,1)} %fusion.4, bf16[9,152,128]{2,0,1:T(8,128)(2,1)S(1)} %fusion.20), kind=kOutput, calls=%fused_computation.9 | convolution fusion | flops 2869952512 | bytes 24860672 | tf_op jit(solution)/shard_map/ikwx,kwt->itx/dot_general | solution.py:85
  77.2 5.1 broadcast_in_dim.18.clone.1
  82.3 5.8 %scatter_fusion.1 = bf16[1024,32,128]{2,0,1:T(8,128)(2,1)} fusion(bf16[1024,32,128]{2,0,1:T(8,128)(2,1)} %broadcast_in_dim.18.clone.1, s32[8]{0:T(128)S(1)} %fusion.61, bf16[8,1024,128]{2,1,0:T(8,128)(2,1)} %bitcast.249), kind=kCustom, calls=%fused_computation.2 | custom fusion | bytes 6291488 | tf_op jit(solution)/shard_map/scatter | solution.py:128
  88.1 8.2 %all-to-all-start.1 = ((bf16[1024,32,128]{2,0,1:T(8,128)(2,1)}), bf16[1024,32,128]{2,0,1:T(8,128)(2,1)}, u32[]{:S(2)}, u32[]{:S(2)}) async-start(bf16[1024,32,128]{2,0,1:T(8,128)(2,1)} %scatter_fusion.1), calls=%async_computation.1 | async-start | bytes 16777216 | tf_op jit(solution)/shard_map/all_to_all | solution.py:136
  101.1 4.5 compare_select_fusion.2
  107.1 4.4 compare_select_fusion.1
  111.5 17.3 %fusion.49 = pred[8,128]{1,0:T(8,128)(4,1)S(1)} fusion(pred[1024]{0:T(1024)(128)(4,1)S(1)} %compare_reduce_fusion, pred[1024]{0:T(1024)(128)(4,1)S(1)} %compare_reduce_fusion.1, pred[1024]{0:T(1024)(128)(4,1)S(1)} %compare_reduce_fusion.2, pred[1024]{0:T(1024)(128)(4,1)S(1)} %compare_reduce_fusion.3, pred[1024]{0:T(1024)(128)(4,1)S(1)} %compare_reduce_fusion.4, ...), kind=kLoop, calls=%fused_computation.147 | loop fusion | flops 39936 | bytes 33904 | tf_op jit(solution)/shard_map/eq | solution.py:55
  128.8 17.6 %fusion.46 = pred[1024]{0:T(1024)(128)(4,1)S(1)} fusion(pred[1024]{0:T(1024)(128)(4,1)S(1)} %compare_reduce_fusion, pred[1024]{0:T(1024)(128)(4,1)S(1)} %compare_reduce_fusion.1, pred[1024]{0:T(1024)(128)(4,1)S(1)} %compare_reduce_fusion.2, pred[1024]{0:T(1024)(128)(4,1)S(1)} %compare_reduce_fusion.3, pred[1024]{0:T(1024)(128)(4,1)S(1)} %compare_reduce_fusion.4, ...), kind=kLoop, calls=%fused_computation.144 | loop fusion | flops 37888 | bytes 33904 | tf_op jit(solution)/shard_map/eq | solution.py:55
  148.5 5.1 broadcast_in_dim.18.clone
  153.6 5.7 %scatter_fusion = bf16[1024,32,128]{2,0,1:T(8,128)(2,1)} fusion(bf16[1024,32,128]{2,0,1:T(8,128)(2,1)} %broadcast_in_dim.18.clone, s32[8]{0:T(128)S(1)} %fusion.61, bf16[8,1024,128]{2,1,0:T(8,128)(2,1)} %fusion.16), kind=kCustom, calls=%fused_computation.1 | custom fusion | bytes 6291488 | tf_op jit(solution)/shard_map/scatter | solution.py:131
  159.3 61.3 %all-to-all-done.1 = bf16[1024,32,128]{2,0,1:T(8,128)(2,1)} async-done(((bf16[1024,32,128]{2,0,1:T(8,128)(2,1)}), bf16[1024,32,128]{2,0,1:T(8,128)(2,1)}, u32[]{:S(2)}, u32[]{:S(2)}) %all-to-all-start.1) | async-done | bytes 8388640 | tf_op jit(solution)/shard_map/all_to_all | solution.py:136
  220.6 5.8 %all-to-all-start = ((bf16[1024,32,128]{2,0,1:T(8,128)(2,1)}), bf16[1024,32,128]{2,0,1:T(8,128)(2,1)}, u32[]{:S(2)}, u32[]{:S(2)}) async-start(bf16[1024,32,128]{2,0,1:T(8,128)(2,1)} %scatter_fusion), calls=%async_computation | async-start | bytes 16777216 | tf_op jit(solution)/shard_map/all_to_all | solution.py:137
  227.5 123.2 %all-to-all-done = bf16[1024,32,128]{2,0,1:T(8,128)(2,1)} async-done(((bf16[1024,32,128]{2,0,1:T(8,128)(2,1)}), bf16[1024,32,128]{2,0,1:T(8,128)(2,1)}, u32[]{:S(2)}, u32[]{:S(2)}) %all-to-all-start) | async-done | bytes 8388640 | tf_op jit(solution)/shard_map/all_to_all | solution.py:137
  350.7 9.0 %convert_reduce_fusion = (f32[1024,128]{1,0:T(8,128)S(1)}, f32[1024,128]{1,0:T(8,128)S(1)}) fusion(bf16[1024,32,128]{2,0,1:T(8,128)(2,1)} %all-to-all-done, bf16[1024,32,128]{2,0,1:T(8,128)(2,1)} %all-to-all-done.1), kind=kLoop, calls=%fused_computation.3 | loop fusion | flops 20709376 | bytes 17825792 | tf_op jit(solution)/shard_map/reduce_sum | solution.py:93
  363.4 2.4 collective-permute-done
  366.8 13.8 %all_to_all.20 = f32[4,256,128]{2,1,0:T(8,128)S(1)} all-to-all(f32[4,256,128]{2,1,0:T(8,128)S(1)} %bitcast.254), channel_id=1, replica_groups=mesh['sky'=32,'band'=4] {'band'}, dimensions={0} | all-to-all | bytes 1048576 | tf_op jit(solution)/shard_map/all_to_all | solution.py:34
  380.5 5.1 stack.134
  385.6 5.7 %all-to-all-start.2 = ((bf16[32,1024,128]{2,1,0:T(8,128)(2,1)}), bf16[32,1024,128]{2,1,0:T(8,128)(2,1)}, u32[]{:S(2)}, u32[]{:S(2)}) async-start(bf16[32,1024,128]{2,1,0:T(8,128)(2,1)} %stack.134), calls=%async_computation.2 | async-start | bytes 16777216 | tf_op jit(solution)/shard_map/all_to_all | solution.py:99
  391.4 3.0 copy.58
  395.2 120.5 %all-to-all-done.2 = bf16[32,1024,128]{2,1,0:T(8,128)(2,1)} async-done(((bf16[32,1024,128]{2,1,0:T(8,128)(2,1)}), bf16[32,1024,128]{2,1,0:T(8,128)(2,1)}, u32[]{:S(2)}, u32[]{:S(2)}) %all-to-all-start.2) | async-done | bytes 8388640 | tf_op jit(solution)/shard_map/all_to_all | solution.py:99
  515.6 5.5 %gather_fusion = bf16[8,1024,128]{2,1,0:T(8,128)(2,1)} fusion(bf16[1024,32,128]{2,0,1:T(8,128)(2,1)} %bitcast.108, s32[1024]{0:T(1024)S(1)} %pad_clamp_fusion), kind=kCustom, calls=%fused_computation | custom fusion | bytes 4194336 | tf_op jit(solution)/shard_map/jit(_take)/gather | solution.py:101
  521.2 2.9 copy.57
  524.0 4.1 subtract_convert_fusion
  528.1 3.9 copy.59
  (90 shorter events, 29.0 us)
Async XLA Ops:
  0.6 76.4 %copy-start = (s32[32,4,8]{0,2,1:T(8,128)S(1)}, s32[32,4,8]{0,2,1:T(8,128)}, u32[]{:S(2)}) copy-start(s32[32,4,8]{0,2,1:T(8,128)} %param.11) | copy-start | bytes 12292
  3.8 0.7 copy-start.4
  3.8 0.7 copy-start.5
  38.9 8.2 %copy-start.2 = (bf16[9,1024,1024]{2,1,0:T(8,128)(2,1)S(1)}, bf16[9,1024,1024]{2,1,0:T(8,128)(2,1)}, u32[]{:S(2)}) copy-start(bf16[9,1024,1024]{2,1,0:T(8,128)(2,1)} %copy.47) | copy-start | bytes 56623108
  61.8 2.4 copy-start.6
  88.1 132.4 %all-to-all-start.1 = ((bf16[1024,32,128]{2,0,1:T(8,128)(2,1)}), bf16[1024,32,128]{2,0,1:T(8,128)(2,1)}, u32[]{:S(2)}, u32[]{:S(2)}) async-start(bf16[1024,32,128]{2,0,1:T(8,128)(2,1)} %scatter_fusion.1), calls=%async_computation.1 | async-start | bytes 16777216 | tf_op jit(solution)/shard_map/all_to_all | solution.py:136
  96.3 3.4 copy-start.3
  220.6 130.2 %all-to-all-start = ((bf16[1024,32,128]{2,0,1:T(8,128)(2,1)}), bf16[1024,32,128]{2,0,1:T(8,128)(2,1)}, u32[]{:S(2)}, u32[]{:S(2)}) async-start(bf16[1024,32,128]{2,0,1:T(8,128)(2,1)} %scatter_fusion), calls=%async_computation | async-start | bytes 16777216 | tf_op jit(solution)/shard_map/all_to_all | solution.py:137
  227.5 134.3 %copy-start.7 = (f32[1,31]{1,0:T(1,128)S(1)}, f32[1,31]{1,0:T(1,128)}, u32[]{:S(2)}) copy-start(f32[1,31]{1,0:T(1,128)} %param.15) | copy-start | bytes 376
  360.0 5.9 %collective-permute-start = (bf16[1024,15]{1,0:T(8,128)(2,1)S(1)}, bf16[1024,15]{1,0:T(8,128)(2,1)S(1)}, u32[]{:S(2)}, u32[]{:S(2)}) collective-permute-start(bf16[1024,15]{1,0:T(8,128)(2,1)S(1)} %get-tuple-element.8), channel_id=1, source_target_pairs={{0,4},{4,8},{8,12},{12,16},{16,20},{20,24},{24,28},{28,32},{32,36}... | collective-permute-start | bytes 92168 | tf_op jit(solution)/shard_map/ppermute | solution.py:18
  360.1 5.8 %collective-permute-start.1 = (bf16[1024,15]{1,0:T(8,128)(2,1)S(1)}, bf16[1024,15]{1,0:T(8,128)(2,1)S(1)}, u32[]{:S(2)}, u32[]{:S(2)}) collective-permute-start(bf16[1024,15]{1,0:T(8,128)(2,1)S(1)} %get-tuple-element.9), channel_id=1, source_target_pairs={{4,0},{8,4},{12,8},{16,12},{20,16},{24,20},{28,24},{32,28},{36,32}... | collective-permute-start | bytes 92168 | tf_op jit(solution)/shard_map/ppermute | solution.py:21
  385.6 130.0 %all-to-all-start.2 = ((bf16[32,1024,128]{2,1,0:T(8,128)(2,1)}), bf16[32,1024,128]{2,1,0:T(8,128)(2,1)}, u32[]{:S(2)}, u32[]{:S(2)}) async-start(bf16[32,1024,128]{2,1,0:T(8,128)(2,1)} %stack.134), calls=%async_computation.2 | async-start | bytes 16777216 | tf_op jit(solution)/shard_map/all_to_all | solution.py:99
  524.0 8.1 %copy-start.1 = (s32[32,4,8]{0,2,1:T(8,128)S(1)}, s32[32,4,8]{0,2,1:T(8,128)}, u32[]{:S(2)}) copy-start(s32[32,4,8]{0,2,1:T(8,128)} %param.11) | copy-start | bytes 12292
